TPU v7x, 256 devices: a whole 4x4x8 slice. The times are simulated.
256 devices in a mesh: wide: 32 (over y, x, core), narrow: 8 (over z).
Axes of the slice: x: 4, y: 4, z: 8, core: 2. Of those that a mesh axis runs over, the one named last changes fastest.
Arguments:
- three_centre: float32 [128, 2048, 1024], P(None, 'wide', 'narrow'), may hold values from -6 to 6
- screen_mask: int32 [128, 16, 8], P('wide', None, 'narrow'), may hold values 0 or 1
- metric: bfloat16 [1024, 1024], P(None, 'narrow'), may hold values from -0.1875 to 0.1875
Outputs:
- contracted: float32 [128, 2048, 1024], P('wide', None, 'narrow')
All inputs are finite; a program needn't handle non-finite values. No bound on the sum of `screen_mask` on one device may be relied on, other than what follows from the above.
Results may differ from a plain program's by a relative error of at most 0.0029.
Values may be sent and summed in bfloat16 or wider, within the bound.
A program may use at most 64 MiB of HBM per device.

v0:
```python
import jax
import jax.numpy as jnp
from jax import lax
from jax.sharding import PartitionSpec as P


def per_device(three_centre, screen_mask, metric):
    nub_all = screen_mask.shape[1]
    auxb_local = screen_mask.shape[2]
    remapped = lax.all_to_all(
        three_centre.astype(jnp.bfloat16), "wide", split_axis=0, concat_axis=1, tiled=True
    ).astype(three_centre.dtype)
    mu_local, nu_all, aux_local = remapped.shape
    block_rows = nu_all // nub_all
    block_cols = aux_local // auxb_local
    blocks = remapped.reshape(mu_local, nub_all, block_rows, auxb_local, block_cols)
    weights = screen_mask[:, :, None, :, None].astype(jnp.float32)
    screened = (blocks * weights).reshape(mu_local, nu_all, aux_local).astype(jnp.bfloat16)
    initial = jnp.zeros((mu_local, nu_all, metric.shape[1]), jnp.float32)
    piece = lax.all_gather(screened, "narrow", axis=2, tiled=True)
    flat = piece.reshape(-1, piece.shape[2])
    product = jnp.dot(flat, metric, preferred_element_type=jnp.float32)
    return product.reshape(initial.shape)


def solution(mesh):
    in_specs = (P(None, "wide", "narrow"), P("wide", None, "narrow"), P(None, "narrow"))
    out_specs = P("wide", None, "narrow")
    return jax.shard_map(
        per_device, mesh=mesh, in_specs=in_specs, out_specs=out_specs, check_vma=False
    )
```

profile of v0, /device:TPU:2, one launch (start us, length us, event | category | flops | bytes accessed | tf_op | source)
XLA Modules:
  0.0 246.3 jit_solution(7557963478260871547)
XLA Ops:
  6.5 0.0 copy-start
  6.5 0.0 copy-start.1
  6.5 4.1 %convert_element_type.32 = bf16[128,64,128]{2,1,0:T(8,128)(2,1)} convert(f32[128,64,128]{2,1,0:T(8,128)} %param.3) | non-fusion elementwise | flops 1048576 | bytes 6291456 | tf_op jit(solution)/shard_map/convert_element_type | solution.py:11
  10.6 7.6 %all-to-all-start = ((bf16[128,64,128]{2,1,0:T(8,128)(2,1)}), bf16[128,64,128]{2,1,0:T(8,128)(2,1)S(1)}, u32[]{:S(2)}, u32[]{:S(2)}) async-start(bf16[128,64,128]{2,1,0:T(8,128)(2,1)} %convert_element_type.32), calls=%async_computation | async-start | bytes 4194304 | tf_op jit(solution)/shard_map/all_to_all | solution.py:10
  18.2 0.0 all-gather.2.cloned.1.call-start
  18.3 0.0 copy-done.1
  18.3 0.1 broadcast_bitcast_fusion
  18.4 27.7 %all-to-all-done = bf16[128,64,128]{2,1,0:T(8,128)(2,1)S(1)} async-done(((bf16[128,64,128]{2,1,0:T(8,128)(2,1)}), bf16[128,64,128]{2,1,0:T(8,128)(2,1)S(1)}, u32[]{:S(2)}, u32[]{:S(2)}) %all-to-all-start) | async-done | bytes 2097184 | tf_op jit(solution)/shard_map/all_to_all | solution.py:10
  46.1 0.4 copy.4
  46.6 2.5 %fusion = bf16[4,2048,128]{2,1,0:T(8,128)(2,1)} fusion(f32[32,4,64,128]{3,2,0,1:T(8,128)S(1)} %copy.4, f32[4,2048]{1,0:T(4,128)S(1)} %bitcast.19), kind=kLoop, calls=%fused_computation.1 | loop fusion | flops 2097152 | bytes 6324224 | tf_op jit(solution)/shard_map/convert_element_type | solution.py:18
  49.1 0.0 all-gather.2.cloned.1.call-update
  49.1 180.2 %all-gather.2.cloned.1.call-done = bf16[4,2048,1024]{2,1,0:T(8,128)(2,1)} async-done(((bf16[4,2048,128]{2,1,0:T(8,128)(2,1)}), bf16[4,2048,1024]{2,1,0:T(8,128)(2,1)}) %all-gather.2.cloned.1.call-update) | async-done | bytes 16777232 | tf_op jit(solution)/shard_map/all_gather | solution.py:20
  229.3 0.0 copy-done
  229.3 10.1 %fusion.1 = f32[4,2048,128]{2,1,0:T(8,128)} fusion(bf16[4,2048,1024]{2,1,0:T(8,128)(2,1)} %all-gather.2.cloned.1.call-done, bf16[1024,128]{1,0:T(8,128)(2,1)S(1)} %copy-done), kind=kOutput, calls=%fused_computation.2 | convolution fusion | flops 2147483648 | bytes 21233664 | tf_op jit(solution)/shard_map/dot_general | solution.py:22
  (2 shorter events, 0.0 us)
Async XLA Ops:
  6.5 222.8 %copy-start = (bf16[1024,128]{1,0:T(8,128)(2,1)S(1)}, bf16[1024,128]{1,0:T(8,128)(2,1)}, u32[]{:S(2)}) copy-start(bf16[1024,128]{1,0:T(8,128)(2,1)} %param.5) | copy-start | bytes 786436
  6.5 11.7 %copy-start.1 = (s32[4,16,1]{1,2,0:T(1,128)S(1)}, s32[4,16,1]{1,2,0:T(1,128)}, u32[]{:S(2)}) copy-start(s32[4,16,1]{1,2,0:T(1,128)} %param.4) | copy-start | bytes 772
  10.6 35.5 %all-to-all-start = ((bf16[128,64,128]{2,1,0:T(8,128)(2,1)}), bf16[128,64,128]{2,1,0:T(8,128)(2,1)S(1)}, u32[]{:S(2)}, u32[]{:S(2)}) async-start(bf16[128,64,128]{2,1,0:T(8,128)(2,1)} %convert_element_type.32), calls=%async_computation | async-start | bytes 4194304 | tf_op jit(solution)/shard_map/all_to_all | solution.py:10
  18.2 211.1 %all-gather.2.cloned.1.call-start = ((), (), s32[]{:S(2)}) async-start(), calls=%async_computation.1 | async-start | bytes 18874368 | tf_op jit(solution)/shard_map/all_gather | solution.py:20
Sparse Core Ops, SparseCore 0:
  49.2 180.0 all-gather.1
where the time goes:
time: 246 us
  waiting for transfers between devices  208 us (85%)
  between operations  13.4 us (5%)
  matrix products  10.1 us (4%)
  starting transfers between devices  7.66 us (3%)
  other arithmetic  6.57 us (3%)
    all_gather x1, waiting for transfers between devices, per_device(): piece = lax.all_gather(screened, 'narrow', axis=2, tiled=True)  180 us
    all_to_all x1, waiting for transfers between devices, per_device(): lax.all_to_all(three_centre.astype(jnp.bfloat16), 'wide', split_axis=0, c...  27.7 us
    dot_general x1, matrix products, per_device(): product = jnp.dot(flat, metric, preferred_element_type=jnp.float32)  10.1 us
    all_to_all x1, starting transfers between devices, per_device(): lax.all_to_all(three_centre.astype(jnp.bfloat16), 'wide', split_axis=0, c...  7.62 us
  transfers between devices with their start and end apart: 2, of which 2 were waited for; matrix products, arithmetic and copies ran while one was open for 0% of the time, Pallas kernels for 0%

commit v1 on v0

--- a/solution.py
+++ b/solution.py
@@ -2,6 +2,7 @@
 import jax.numpy as jnp
 from jax import lax
 from jax.sharding import PartitionSpec as P
+from jax.lax import all_to_all, axis_size
 
 
 def per_device(three_centre, screen_mask, metric):
@@ -17,7 +18,10 @@
     weights = screen_mask[:, :, None, :, None].astype(jnp.float32)
     screened = (blocks * weights).reshape(mu_local, nu_all, aux_local).astype(jnp.bfloat16)
     initial = jnp.zeros((mu_local, nu_all, metric.shape[1]), jnp.float32)
-    piece = lax.all_gather(screened, "narrow", axis=2, tiled=True)
+    near = tuple((screened for _ in range(axis_size("narrow"))))
+    latest = jnp.stack(near, axis=0)
+    all_rows = all_to_all(latest, "narrow", 0, 0)
+    piece = jnp.concatenate(all_rows, 2)
     flat = piece.reshape(-1, piece.shape[2])
     product = jnp.dot(flat, metric, preferred_element_type=jnp.float32)
     return product.reshape(initial.shape)

time: 246 us -> 425 us (1.73)
  blocking collectives: 0 us -> 374 us
  waiting for transfers between devices: 208 us -> 27.8 us
  between operations: 13.4 us -> 0.07 us
    all_to_all x0 -> x1, blocking collectives: none -> 374 us  [per_device(): all_rows = all_to_all(latest, 'narrow', 0, 0)]
    all_gather x1 -> x0, waiting for transfers between devices: 180 us -> none  [per_device(): piece = lax.all_gather(screened, 'narrow', axis=2, tiled=True)]
  transfers between devices with their start and end apart: 2 -> 1, of which waited for: 2 -> 1; matrix products, arithmetic and copies ran while one was open for 0% -> 0% of each run, Pallas kernels for 0% -> 0%
where the time goes in v1:
time: 425 us; the launch traced here: 424 us
  blocking collectives  374 us (88%)
  waiting for transfers between devices  27.8 us (7%)
  starting transfers between devices  7.62 us (2%)
  matrix products  6.1 us (1%)
  other arithmetic  5.97 us (1%)
    all_to_all x1, blocking collectives, per_device(): all_rows = all_to_all(latest, 'narrow', 0, 0)  374 us
    all_to_all x1, waiting for transfers between devices, per_device(): lax.all_to_all(three_centre.astype(jnp.bfloat16), 'wide', split_axis=0, c...  27.8 us
  transfers between devices with their start and end apart: 1, of which 1 were waited for; matrix products, arithmetic and copies ran while one was open for 0% of the time, Pallas kernels for 0%

profile of v1, /device:TPU:2, one launch (start us, length us, event | category | flops | bytes accessed | tf_op | source)
XLA Modules:
  0.0 424.2 jit_solution(14761576869081528431)
XLA Ops:
  0.0 0.0 copy-start
  0.0 0.0 copy-start.1
  0.0 4.1 convert_element_type.36
  4.1 7.6 %all-to-all-start = ((bf16[128,64,128]{2,1,0:T(8,128)(2,1)}), bf16[128,64,128]{2,1,0:T(8,128)(2,1)S(1)}, u32[]{:S(2)}, u32[]{:S(2)}) async-start(bf16[128,64,128]{2,1,0:T(8,128)(2,1)} %convert_element_type.36), calls=%async_computation | async-start | bytes 4194304 | tf_op jit(solution)/shard_map/all_to_all | solution.py:11
  11.7 0.0 copy-done.1
  11.7 0.1 broadcast_bitcast_fusion
  11.8 27.8 %all-to-all-done = bf16[128,64,128]{2,1,0:T(8,128)(2,1)S(1)} async-done(((bf16[128,64,128]{2,1,0:T(8,128)(2,1)}), bf16[128,64,128]{2,1,0:T(8,128)(2,1)S(1)}, u32[]{:S(2)}, u32[]{:S(2)}) %all-to-all-start) | async-done | bytes 2097184 | tf_op jit(solution)/shard_map/all_to_all | solution.py:11
  39.6 0.5 convert_bitcast_fusion
  40.1 0.6 copy.5
  40.7 1.4 fusion.3
  42.1 2.3 stack.2
  44.4 373.7 %all_to_all.14 = bf16[8,4,2048,128]{3,2,1,0:T(8,128)(2,1)S(1)} all-to-all(bf16[8,4,2048,128]{3,2,1,0:T(8,128)(2,1)S(1)} %stack.2), channel_id=1, replica_groups=mesh['wide'=32,'narrow'=8] {'narrow'}, dimensions={0} | all-to-all | bytes 33554432 | tf_op jit(solution)/shard_map/all_to_all | solution.py:23
  418.1 0.0 copy-done
  418.1 6.1 %fusion = f32[4,2048,128]{2,1,0:T(8,128)} fusion(bf16[1024,128]{1,0:T(8,128)(2,1)S(1)} %copy-done, bf16[8,4,2048,128]{3,2,1,0:T(8,128)(2,1)S(1)} %all_to_all.14), kind=kOutput, calls=%fused_computation | convolution fusion | flops 2147483648 | bytes 21233664 | tf_op jit(solution)/shard_map/dot_general | solution.py:26
  (2 shorter events, 0.0 us)
Async XLA Ops:
  0.0 418.1 %copy-start = (bf16[1024,128]{1,0:T(8,128)(2,1)S(1)}, bf16[1024,128]{1,0:T(8,128)(2,1)}, u32[]{:S(2)}) copy-start(bf16[1024,128]{1,0:T(8,128)(2,1)} %param.5) | copy-start | bytes 786436
  0.0 11.7 %copy-start.1 = (s32[4,16,1]{1,2,0:T(1,128)S(1)}, s32[4,16,1]{1,2,0:T(1,128)}, u32[]{:S(2)}) copy-start(s32[4,16,1]{1,2,0:T(1,128)} %param.4) | copy-start | bytes 772
  4.1 35.5 %all-to-all-start = ((bf16[128,64,128]{2,1,0:T(8,128)(2,1)}), bf16[128,64,128]{2,1,0:T(8,128)(2,1)S(1)}, u32[]{:S(2)}, u32[]{:S(2)}) async-start(bf16[128,64,128]{2,1,0:T(8,128)(2,1)} %convert_element_type.36), calls=%async_computation | async-start | bytes 4194304 | tf_op jit(solution)/shard_map/all_to_all | solution.py:11
